TPU v7x, 32 devices: a whole 2x2x4 slice. The times are simulated.
32 devices in a mesh: blk: 8 (over z, x), tile: 4 (over y, core).
Axes of the slice: x: 2, y: 2, z: 4, core: 2. Of those that a mesh axis runs over, the one named last changes fastest.
Arguments:
- stream_in: bfloat16 [32, 16, 16, 2240], P('tile', 'blk'), may hold values from -6 to 6
- queries: bfloat16 [32, 16, 16, 2240], P('tile', 'blk'), may hold values from -12 to 12
- key_rows: bfloat16 [32, 16, 16, 2240], P('tile', 'blk'), may hold values from -12 to 12
- value_rows: bfloat16 [32, 16, 16, 2240], P('tile', 'blk'), may hold values from -12 to 12
- w_output: bfloat16 [2240, 2240], P('tile'), may hold values from -0.125 to 0.125
- w_inner: bfloat16 [2240, 2, 4096], P(None, None, 'tile'), may hold values from -0.125 to 0.125
- w_down: bfloat16 [4096, 2240], P('tile'), may hold values from -0.09375 to 0.09375
- spatial_taps: float32 [3, 3, 2, 4096], P(None, None, None, 'tile'), may hold values from -2 to 2
- temporal_taps: float32 [3, 2, 4096], P(None, None, 'tile'), may hold values from -3.5 to 3.5
Outputs:
- layer_out: bfloat16 [32, 16, 16, 2240], P('tile', 'blk')
All inputs are finite; a program needn't handle non-finite values.
Results may differ from a plain program's by a relative error of at most 0.009.
Values may be sent and summed in bfloat16 or wider, within the bound.
A program may use at most 128 MiB of HBM per device.

v0:
```python
import jax
import jax.numpy as jnp
from jax import lax
from jax.sharding import PartitionSpec as P

HEADS = 20
HEAD_DIM = 112
TAPS = 3
EPS = 1e-06


def from_partner(value, axis, stride):
    mask = 2**stride
    pairs = [(source, source ^ mask) for source in range(lax.axis_size(axis))]
    return lax.ppermute(value, axis, pairs)


def carried_in(x, axis, combine, identity):
    peers, position = (lax.axis_size(axis), lax.axis_index(axis))
    everything = jax.tree.map(lambda part: lax.all_gather(part, axis), x)
    start = jax.tree.map(
        lambda part, zero: jnp.broadcast_to(jnp.asarray(zero, part.dtype), part.shape), x, identity
    )

    def step(k, before):
        reached = k < position
        new = combine(before, jax.tree.map(lambda part: part[k], everything))
        return jax.tree.map(lambda a, b: jnp.where(reached, a, b), new, before)

    return lax.fori_loop(0, peers, step, start)


def shifted(x, axis, by):
    peers = lax.axis_size(axis)
    pairs = [(i, i + by) for i in range(peers) if 0 <= i + by < peers]
    return lax.ppermute(x, axis, pairs)


def add_pair(earlier, later):
    return (earlier[0] + later[0], earlier[1] + later[1])


def prefix_state(state_parts):
    partner = from_partner((state_parts[0], state_parts[1]), "blk", 0)
    block_sum = add_pair(state_parts, partner)
    odd_side = (lax.axis_index("blk") % 2).astype(jnp.float32)
    keep_share = 1.0 - 0.5 * odd_side
    zero_state = (jnp.zeros_like(block_sum[0]), jnp.zeros_like(block_sum[1]))
    before = carried_in((block_sum[0] * 0.5, block_sum[1] * 0.5), "blk", add_pair, zero_state)
    return (before[0] + block_sum[0] * keep_share, before[1] + block_sum[1] * keep_share)


def spatial_conv(inner_act, spatial_taps):
    row_count = inner_act.shape[0]
    col_count = inner_act.shape[2]
    padded = jnp.pad(inner_act, ((1, 1), (0, 0), (1, 1), (0, 0), (0, 0)))
    running = jnp.zeros(inner_act.shape, jnp.float32)
    for tap_row in range(3):
        for tap_col in range(3):
            window = padded[tap_row : tap_row + row_count, :, tap_col : tap_col + col_count]
            running = running + window.astype(jnp.float32) * spatial_taps[tap_row, tap_col]
    return running


def on_device(
    stream_in, queries, key_rows, value_rows, w_output, w_inner, w_down, spatial_taps, temporal_taps
):
    row_count, frames, col_count, model_width = queries.shape
    tokens = row_count * frames * col_count
    highest = lax.Precision.HIGHEST
    key_pos = jax.nn.relu(key_rows).reshape(tokens, HEADS, HEAD_DIM)
    value_heads = value_rows.reshape(tokens, HEADS, HEAD_DIM)
    local_kv = jnp.einsum("thd,the->hde", key_pos, value_heads, preferred_element_type=jnp.float32)
    local_kv = local_kv.reshape(model_width, HEAD_DIM)
    local_z = jnp.sum(key_pos.astype(jnp.float32), axis=0).reshape(model_width)
    shares = (
        lax.psum_scatter(local_kv, "tile", scatter_dimension=0, tiled=True),
        lax.psum_scatter(local_z, "tile", scatter_dimension=0, tiled=True),
    )
    share_state = prefix_state(shares)
    state, zsum = (
        lax.all_gather(share_state[0], "tile", axis=0, tiled=True),
        lax.all_gather(share_state[1], "tile", axis=0, tiled=True),
    )
    state = state.reshape(HEADS, HEAD_DIM, HEAD_DIM)
    zsum = zsum.reshape(HEADS, HEAD_DIM)
    query_pos = jax.nn.relu(queries.astype(jnp.float32)).reshape(tokens, HEADS, HEAD_DIM)
    numerator = jnp.einsum("thd,hde->the", query_pos, state, precision=highest)
    denominator = jnp.einsum("thd,hd->th", query_pos, zsum, precision=highest) + EPS
    attended = (numerator / denominator[..., None]).astype(jnp.bfloat16)
    attended = attended.reshape(row_count, frames, col_count, model_width)
    by_feature = lax.all_to_all(attended, "tile", split_axis=3, concat_axis=0, tiled=True)
    portion = by_feature
    product = jnp.dot(
        portion.reshape(-1, portion.shape[3]), w_output, preferred_element_type=jnp.float32
    )
    attn_out = lax.psum_scatter(
        product.reshape(row_count * lax.axis_size("tile"), frames, col_count, model_width),
        "tile",
        scatter_dimension=0,
        tiled=True,
    )
    hidden = (stream_in.astype(jnp.float32) + attn_out).astype(jnp.bfloat16)
    chan_dev = w_inner.shape[2]
    w_flat = w_inner.reshape(model_width, 2 * chan_dev)
    portion = lax.all_gather(hidden, "tile", axis=0, tiled=True)
    product = jnp.dot(portion.reshape(-1, model_width), w_flat, preferred_element_type=jnp.float32)
    activated = jax.nn.silu(product).astype(jnp.bfloat16)
    inner_act = activated.reshape(portion.shape[0], frames, col_count, 2, chan_dev)
    spatial = spatial_conv(inner_act, spatial_taps).astype(jnp.bfloat16)
    earlier_frames = shifted(spatial, "blk", 1)
    extended = jnp.concatenate([earlier_frames, spatial], axis=1)
    temporal_mix = jnp.zeros(spatial.shape, jnp.float32)
    for lag in range(TAPS):
        window = extended[:, TAPS - 1 - lag : TAPS - 1 - lag + frames]
        temporal_mix = temporal_mix + window.astype(jnp.float32) * temporal_taps[lag]
    gated_out = (temporal_mix[..., 0, :] * jax.nn.silu(temporal_mix[..., 1, :])).astype(
        jnp.bfloat16
    )
    portion = gated_out
    product = jnp.dot(portion.reshape(-1, chan_dev), w_down, preferred_element_type=jnp.float32)
    ffn_out = lax.psum_scatter(
        product.reshape(lax.axis_size("tile") * row_count, frames, col_count, model_width).astype(
            jnp.bfloat16
        ),
        "tile",
        scatter_dimension=0,
        tiled=True,
    ).astype(jnp.float32)
    return (hidden.astype(jnp.float32) + ffn_out).astype(jnp.bfloat16)


def solution(mesh):
    in_specs = (
        P("tile", "blk", None, None),
        P("tile", "blk", None, None),
        P("tile", "blk", None, None),
        P("tile", "blk", None, None),
        P("tile", None),
        P(None, None, "tile"),
        P("tile", None),
        P(None, None, None, "tile"),
        P(None, None, "tile"),
    )
    out_specs = P("tile", "blk", None, None)
    return jax.shard_map(
        on_device, mesh=mesh, in_specs=in_specs, out_specs=out_specs, check_vma=False
    )
```

profile of v0, /device:TPU:0, one launch (start us, length us, event | category | flops | bytes accessed | tf_op | source)
XLA Modules:
  0.0 571.9 jit_solution(4636084456415027600)
XLA Ops:
  6.5 2.5 broadcast_maximum_fusion
  9.1 4.0 reshape.58
  13.1 4.0 reshape.59
  17.1 3.5 fusion.8
  20.6 0.0 all-gather.7.cloned.1.call-start
  20.6 28.2 %reduce-scatter.4.cloned.1.call-done = f32[560,112]{1,0:T(8,128)} async-done(((f32[2240,112]{1,0:T(8,128)}), f32[560,112]{1,0:T(8,128)}) %reduce-scatter.4.cloned.1.call-update) | async-done | bytes 250896 | tf_op jit(solution)/shard_map/reduce_scatter | solution.py:77
  48.9 1.5 collective-permute-start
  50.3 7.2 %collective-permute-done = f32[560,112]{1,0:T(8,128)S(1)} collective-permute-done((f32[560,112]{1,0:T(8,128)}, f32[560,112]{1,0:T(8,128)S(1)}, u32[]{:S(2)}, u32[]{:S(2)}) %collective-permute-start) | collective-permute-done | bytes 250912 | tf_op jit(solution)/shard_map/ppermute | solution.py:15
  57.5 1.7 broadcast_multiply_fusion
  59.2 0.0 all-gather.7.cloned.1.call-update
  59.3 0.0 reduce-scatter.6.cloned.1.call-start
  59.3 0.7 fusion.13
  60.6 1.5 convert_reduce_fusion
  62.2 10.2 %all-reduce.3 = f32[2240]{0:T(1024)S(1)} all-reduce(f32[2240]{0:T(1024)S(1)} %convert_reduce_fusion), channel_id=5, replica_groups=mesh['blk'=8,'tile'=4] {'tile'}, use_global_device_ids=true, to_apply=%region_2.3.clone | all-reduce | flops 2240 | bytes 17920
  72.3 0.1 dynamic-slice.3
  72.4 1.9 collective-permute-start.1
  74.3 3.0 convert_maximum_fusion
  77.3 0.6 dynamic-slice
  79.2 4.3 reshape.62
  83.5 3.3 copy.27
  86.8 0.2 multiply_dynamic-update-slice_fusion
  87.0 36.8 %all-reduce.1 = f32[4480]{0:T(1024)S(1)} all-reduce(f32[4480]{0:T(1024)S(1)} %multiply_dynamic-update-slice_fusion), channel_id=3, replica_groups=mesh['blk'=8,'tile'=4] {'blk'}, use_global_device_ids=true, to_apply=%add.1 | all-reduce | flops 4480 | bytes 35840
  123.8 0.1 reshape.69
  123.9 0.0 all-gather.7.cloned.1.call-done
  123.9 8.9 %while.16 = (s32[]{:T(128)}, f32[560,112]{1,0:T(8,128)S(1)}, f32[560]{0:T(1024)S(1)}, s32[]{:T(128)}, f32[8,560,112]{2,1,0:T(8,128)}, /*index=5*/f32[8,560]{1,0:T(8,128)S(1)}, s32[]{:T(128)}, s32[]{:T(128)}) while((s32[]{:T(128)}, f32[560,112]{1,0:T(8,128)S(1)}, f32[560]{0:T(1024)S(1)}, s32[]{:T(128)}, f32[8,560,112]{2,1,0:T(8,128)}, ...), condition=%wide.region_4.5_spmd.clone, body=%wide.region_3.4_spmd.clone.sunk | while | flops 189844 | bytes 763955 | solution.py:30
  123.9 1.0 add_select_fusion.4
  125.0 1.0 add_select_fusion.4
  126.1 1.0 add_select_fusion.4
  127.3 1.0 add_select_fusion.4
  128.4 1.0 add_select_fusion.4
  129.5 1.0 add_select_fusion.4
  130.6 1.0 add_select_fusion.4
  131.7 1.0 add_select_fusion.4
  132.8 0.2 add_dynamic-update-slice_fusion
  133.0 10.1 %all-reduce.2 = f32[2240]{0:T(1024)S(1)} all-reduce(f32[2240]{0:T(1024)S(1)} %add_dynamic-update-slice_fusion), channel_id=1, replica_groups=mesh['blk'=8,'tile'=4] {'tile'}, use_global_device_ids=true, to_apply=%add.2 | all-reduce | flops 2240 | bytes 17920
  143.1 0.1 reshape.85
  143.2 3.0 fusion.14
  146.2 0.1 multiply_add_fusion.1
  146.3 9.7 %all_gather.25 = f32[2240,112]{1,0:T(8,128)S(1)} all-gather(f32[560,112]{1,0:T(8,128)S(1)} %multiply_add_fusion.1), channel_id=1, replica_groups=mesh['blk'=8,'tile'=4] {'tile'}, dimensions={0}, use_global_device_ids=true | all-gather | bytes 1254400 | tf_op jit(solution)/shard_map/all_gather | solution.py:82
  156.0 3.2 fusion.5
  159.2 28.0 %reshape.86 = bf16[8,2,16,2240]{2,1,0,3:T(2,128)(2,1)} reshape(bf16[256,20,112]{0,2,1:T(8,128)(2,1)} %fusion.5) | data formatting | bytes 2293760 | tf_op jit(solution)/shard_map/reshape | solution.py:91
  187.2 11.8 %reshape.89 = bf16[4,2,71680]{2,1,0:T(2,128)(2,1)} reshape(bf16[2240,8,2,16]{3,2,1,0:T(2,128)(2,1)} %bitcast.90) | data formatting | bytes 2293760
  198.9 19.8 %all_to_all.15 = bf16[4,2,71680]{2,1,0:T(2,128)(2,1)} all-to-all(bf16[4,2,71680]{2,1,0:T(2,128)(2,1)} %reshape.89), channel_id=1, replica_groups=mesh['blk'=8,'tile'=4] {'tile'}, dimensions={0} | all-to-all | bytes 2293760 | tf_op jit(solution)/shard_map/all_to_all | solution.py:92
  218.8 8.7 %reshape.90 = bf16[2240,8,2,16]{3,2,1,0:T(2,128)(2,1)} reshape(bf16[4,2,71680]{2,1,0:T(2,128)(2,1)} %all_to_all.15) | data formatting | bytes 2293760
  227.5 19.9 %copy.30 = bf16[8,2,16,4,560]{4,2,1,0,3:T(8,128)(2,1)} copy(bf16[8,2,16,4,560]{2,1,0,4,3:T(2,128)(2,1)} %bitcast.91) | data formatting | bytes 2293760 | tf_op jit(solution)/shard_map/all_to_all | solution.py:92
  247.3 7.8 %fusion.3 = f32[32,2,16,2240]{3,2,1,0:T(8,128)} fusion(bf16[32,2,16,560]{3,2,1,0:T(8,128)(2,1)} %bitcast.95, bf16[560,2240]{1,0:T(8,128)(2,1)S(1)} %copy-done), kind=kOutput, calls=%fused_computation.21 | convolution fusion | flops 2569011200 | bytes 12830720 | tf_op jit(solution)/shard_map/dot_general | solution.py:94
  255.2 0.0 reduce-scatter.6.cloned.1.call-update
  255.2 0.0 all-gather.5.cloned.1.call-start
  255.2 74.2 %reduce-scatter.6.cloned.1.call-done = f32[8,2,16,2240]{3,2,1,0:T(8,128)} async-done(((f32[32,2,16,2240]{3,2,1,0:T(8,128)}), f32[8,2,16,2240]{3,2,1,0:T(8,128)}) %reduce-scatter.6.cloned.1.call-update) | async-done | bytes 2293776 | tf_op jit(solution)/shard_map/reduce_scatter | solution.py:97
  329.4 2.9 add_convert_fusion.2
  332.3 0.0 all-gather.5.cloned.1.call-update
  332.4 0.3 reduce-scatter.8.cloned.1.call-start
  332.6 11.4 %copy.38 = bf16[280,8,2,1024]{3,1,2,0:T(8,128)(2,1)} copy(bf16[280,8,2,1024]{3,2,1,0:T(2,128)(2,1)} %bitcast.92) | data formatting | bytes 18350080
  344.1 25.9 %all-gather.5.cloned.1.call-done = bf16[32,2,16,2240]{3,2,1,0:T(8,128)(2,1)} async-done(((bf16[8,2,16,2240]{3,2,1,0:T(8,128)(2,1)}), bf16[32,2,16,2240]{3,2,1,0:T(8,128)(2,1)}) %all-gather.5.cloned.1.call-update) | async-done | bytes 4587536 | tf_op jit(solution)/shard_map/all_gather | solution.py:106
  370.0 16.0 %multiply_convert_fusion = bf16[1024,2048]{1,0:T(8,128)(2,1)} fusion(bf16[1024,2240]{1,0:T(8,128)(2,1)} %bitcast.98, bf16[2240,2048]{1,0:T(8,128)(2,1)} %bitcast.93), kind=kOutput, calls=%fused_computation.13 | convolution fusion | flops 9405726720 | bytes 17956864 | tf_op jit(solution)/shard_map/dot_general | solution.py:107
  386.0 7.8 %reshape.67 = bf16[32,2,16,2,1024]{4,3,2,1,0:T(2,128)(2,1)} reshape(bf16[1024,2048]{1,0:T(8,128)(2,1)} %multiply_convert_fusion) | data formatting | bytes 8388608 | tf_op jit(solution)/shard_map/reshape | solution.py:109
  393.8 3.5 copy.31
  397.3 11.9 %add_convert_fusion = bf16[32,2,16,2,1024]{4,2,1,0,3:T(8,128)(2,1)S(1)} fusion(bf16[32,2,16,2,1024]{4,2,1,0,3:T(8,128)(2,1)S(1)} %copy.31, f32[2,1024]{1,0:T(2,128)S(1)} %get-tuple-element.157, f32[2,1024]{1,0:T(2,128)S(1)} %get-tuple-element.158, f32[2,1024]{1,0:T(2,128)S(1)} %get-tuple-element.151, f32[2,1024]{1,0:T(2,128)S(1)} %get-tuple-element.152, ...), kind=kLoop, calls=%fused_computation.12 | loop fusion | flops 56623104 | bytes 8462336 | tf_op jit(solution)/shard_map/convert_element_type | solution.py:110
  409.2 3.9 collective-permute-start.2
  413.2 89.7 %collective-permute-done.2 = bf16[32,2,16,2,1024]{4,2,1,0,3:T(8,128)(2,1)S(1)} collective-permute-done((bf16[32,2,16,2,1024]{4,2,1,0,3:T(8,128)(2,1)S(1)}, bf16[32,2,16,2,1024]{4,2,1,0,3:T(8,128)(2,1)S(1)}, u32[]{:S(2)}, u32[]{:S(2)}) %collective-permute-start.2) | collective-permute-done | bytes 4194336 | tf_op jit(solution)/shard_map/ppermute | solution.py:36
  502.8 3.2 multiply_add_fusion
  506.0 7.3 %convolution_convert_fusion = bf16[32,2,16,2240]{3,2,1,0:T(8,128)(2,1)} fusion(bf16[1024,2240]{0,1:T(8,128)(2,1)S(1)} %bitcast.100, f32[32,2,16,2,1024]{4,2,1,0,3:T(8,128)S(1)} %multiply_add_fusion), kind=kOutput, calls=%fused_computation.14 | convolution fusion | flops 4706205696 | bytes 17563648 | tf_op jit(solution)/shard_map/dot_general | solution.py:121
  513.4 49.1 %reduce-scatter.8.cloned.1.call-done = bf16[8,2,16,2240]{3,2,1,0:T(8,128)(2,1)} async-done(((bf16[32,2,16,2240]{3,2,1,0:T(8,128)(2,1)}), bf16[8,2,16,2240]{3,2,1,0:T(8,128)(2,1)}) %reduce-scatter.8.cloned.1.call-update) | async-done | bytes 1146896 | tf_op jit(solution)/shard_map/reduce_scatter | solution.py:122
  562.5 2.9 add_convert_fusion.1
  (50 shorter events, 0.3 us)
Async XLA Ops:
  6.5 240.8 %copy-start = (bf16[560,2240]{1,0:T(8,128)(2,1)S(1)}, bf16[560,2240]{1,0:T(8,128)(2,1)}, u32[]{:S(2)}) copy-start(bf16[560,2240]{1,0:T(8,128)(2,1)} %param.15) | copy-start | bytes 7526404
  6.5 42.3 %reduce-scatter.4.cloned.1.call-start = ((), (), s32[]{:S(2)}) async-start(), calls=%async_computation.4 | async-start | bytes 1433600 | tf_op jit(solution)/shard_map/reduce_scatter | solution.py:77
  13.1 46.2 %copy-start.7 = (u32[32]{0:T(128)S(1)}, u32[32]{0:T(128)}, u32[]{:S(2)}) copy-start(u32[32]{0:T(128)} %constant.77) | copy-start | bytes 388
  20.6 56.7 %copy-start.8 = (u32[32]{0:T(128)S(1)}, u32[32]{0:T(128)}, u32[]{:S(2)}) copy-start(u32[32]{0:T(128)} %constant.72) | copy-start | bytes 388
  20.6 103.3 %all-gather.7.cloned.1.call-start = ((), (), s32[]{:S(2)}) async-start(), calls=%async_computation.8 | async-start | bytes 2580480 | tf_op jit(solution)/shard_map/all_gather | solution.py:20
  48.9 8.6 %collective-permute-start = (f32[560,112]{1,0:T(8,128)}, f32[560,112]{1,0:T(8,128)S(1)}, u32[]{:S(2)}, u32[]{:S(2)}) collective-permute-start(f32[560,112]{1,0:T(8,128)} %reduce-scatter.4.cloned.1.call-done), channel_id=1, source_target_pairs={{0,4},{4,0},{8,12},{12,8},{16,20},{20,16},{24,28},{28,24},{1,5},{5... | collective-permute-start | bytes 752648 | tf_op jit(solution)/shard_map/ppermute | solution.py:15
  59.3 270.2 %reduce-scatter.6.cloned.1.call-start = ((), (), s32[]{:S(2)}) async-start(), calls=%async_computation.5 | async-start | bytes 11796480 | tf_op jit(solution)/shard_map/reduce_scatter | solution.py:97
  72.4 14.4 %collective-permute-start.1 = (f32[560]{0:T(1024)S(1)}, f32[560]{0:T(1024)S(1)}, u32[]{:S(2)}, u32[]{:S(2)}) collective-permute-start(f32[560]{0:T(1024)S(1)} %dynamic-slice.3), channel_id=1, source_target_pairs={{0,4},{4,0},{8,12},{12,8},{16,20},{20,16},{24,28},{28,24},{1,5},{5... | collective-permute-start | bytes 6728 | tf_op jit(solution)/shard_map/ppermute | solution.py:15
  86.8 59.4 %copy-start.4 = (f32[560,112]{1,0:T(8,128)S(1)}, f32[560,112]{1,0:T(8,128)}, u32[]{:S(2)}) copy-start(f32[560,112]{1,0:T(8,128)} %reduce-scatter.4.cloned.1.call-done) | copy-start | bytes 752644
  143.2 12.8 %copy-start.2 = (f32[256,20,112]{0,2,1:T(8,128)S(1)}, f32[256,20,112]{0,2,1:T(8,128)}, u32[]{:S(2)}) copy-start(f32[256,20,112]{0,2,1:T(8,128)} %copy.27) | copy-start | bytes 6881284
  255.2 74.3 %copy-start.3 = (bf16[8,2,16,2240]{3,2,1,0:T(8,128)(2,1)S(1)}, bf16[8,2,16,2240]{3,2,1,0:T(8,128)(2,1)}, u32[]{:S(2)}) copy-start(bf16[8,2,16,2240]{3,2,1,0:T(8,128)(2,1)} %param.11) | copy-start | bytes 3440644
  255.2 114.8 %all-gather.5.cloned.1.call-start = ((), (), s32[]{:S(2)}) async-start(), calls=%async_computation.6 | async-start | bytes 5898240 | tf_op jit(solution)/shard_map/all_gather | solution.py:106
  332.4 230.1 %reduce-scatter.8.cloned.1.call-start = ((), (), s32[]{:S(2)}) async-start(), calls=%async_computation.7 | async-start | bytes 5898240 | tf_op jit(solution)/shard_map/reduce_scatter | solution.py:122
  332.6 11.4 %copy-start.5 = (f32[3,3,2,1024]{3,2,1,0:T(2,128)S(1)}, f32[3,3,2,1024]{3,2,1,0:T(2,128)}, u32[]{:S(2)}) copy-start(f32[3,3,2,1024]{3,2,1,0:T(2,128)} %param.18) | copy-start | bytes 221188
  397.3 15.8 %copy-start.6 = (f32[3,2,1024]{2,1,0:T(2,128)S(1)}, f32[3,2,1024]{2,1,0:T(2,128)}, u32[]{:S(2)}) copy-start(f32[3,2,1024]{2,1,0:T(2,128)} %param.19) | copy-start | bytes 73732
  397.3 108.7 %slice-start = ((s8[4587520]{0:T(1024)(128)(4,1)}), s8[4194304]{0:T(1024)(128)(4,1)S(1)}, s32[]{:S(2)}) async-start(s8[4587520]{0:T(1024)(128)(4,1)} %bitcast.99), calls=%async_computation.9 | async-start | bytes 8388608
  409.2 93.6 %collective-permute-start.2 = (bf16[32,2,16,2,1024]{4,2,1,0,3:T(8,128)(2,1)S(1)}, bf16[32,2,16,2,1024]{4,2,1,0,3:T(8,128)(2,1)S(1)}, u32[]{:S(2)}, u32[]{:S(2)}) collective-permute-start(bf16[32,2,16,2,1024]{4,2,1,0,3:T(8,128)(2,1)S(1)} %add_convert_fusion), channel_id=1, source_target_pairs={{0,4},{4,8},{8,12},{12,16},{16,20},{20,24},{24,28},{1,5},{5,9},{9,... | collective-permute-start | bytes 12582920 | tf_op jit(solution)/shard_map/ppermute | solution.py:36
  502.8 3.2 slice-start.1
  506.0 59.4 %copy-start.1 = (bf16[560,2240]{1,0:T(8,128)(2,1)S(1)}, bf16[560,2240]{1,0:T(8,128)(2,1)}, u32[]{:S(2)}) copy-start(bf16[560,2240]{1,0:T(8,128)(2,1)} %param.15) | copy-start | bytes 7526404
Sparse Core Ops, SparseCore 0:
  20.7 28.1 reduce-scatter.3
  59.4 51.7 all-gather.6
  255.3 74.0 reduce-scatter.5
  332.5 37.4 all-gather.4
  513.5 48.9 reduce-scatter.7
where the time goes:
time: 574 us; the launch traced here: 572 us
  waiting for transfers between devices  274 us (48%)
  local copies, waits for them, and re-layouts  108 us (19%)
  blocking collectives  86.6 us (15%)
  matrix products  40.7 us (7%)
  other arithmetic  38.5 us (7%)
  between operations  15.2 us (3%)
  starting transfers between devices  7.66 us (1%)
    ppermute x1, waiting for transfers between devices, shifted(): return lax.ppermute(x, axis, pairs)  89.7 us
    reduce_scatter x1, waiting for transfers between devices, on_device(): lax.psum_scatter(product.reshape(row_count * lax.axis_size('tile'), frame...  74.2 us
    unnamed x3, blocking collectives  57.1 us
    reduce_scatter x1, waiting for transfers between devices, on_device(): lax.psum_scatter(product.reshape(lax.axis_size('tile') * row_count, frame...  49.1 us
    unnamed x30, local copies, waits for them, and re-layouts  33.3 us
    reduce_scatter x1, waiting for transfers between devices, on_device(): lax.psum_scatter(local_kv, 'tile', scatter_dimension=0, tiled=True)  28.2 us
    reshape x1, local copies, waits for them, and re-layouts, on_device(): attended = attended.reshape(row_count, frames, col_count, model_width)  28 us
    all_gather x1, waiting for transfers between devices, on_device(): portion = lax.all_gather(hidden, 'tile', axis=0, tiled=True)  25.9 us
  transfers between devices with their start and end apart: 8, of which 6 were waited for; matrix products, arithmetic and copies ran while one was open for 4% of the time, Pallas kernels for 0%

commit v1 on v0

--- a/solution.py
+++ b/solution.py
@@ -89,7 +89,15 @@
     denominator = jnp.einsum("thd,hd->th", query_pos, zsum, precision=highest) + EPS
     attended = (numerator / denominator[..., None]).astype(jnp.bfloat16)
     attended = attended.reshape(row_count, frames, col_count, model_width)
-    by_feature = lax.all_to_all(attended, "tile", split_axis=3, concat_axis=0, tiled=True)
+    ways, here = (lax.axis_size("tile"), lax.axis_index("tile"))
+    width = attended.shape[3] // ways
+    turned = jnp.roll(attended, -here * width, axis=3)
+    got = [lax.slice_in_dim(turned, 0, width, axis=3)]
+    for far in range(1, ways):
+        sent = lax.slice_in_dim(turned, far * width, (far + 1) * width, axis=3)
+        got.append(lax.ppermute(sent, "tile", [(d, (d + far) % ways) for d in range(ways)]))
+    line = jnp.concatenate(got[::-1], axis=0)
+    by_feature = jnp.roll(line, (here + 1) * got[0].shape[0], axis=0)
     portion = by_feature
     product = jnp.dot(
         portion.reshape(-1, portion.shape[3]), w_output, preferred_element_type=jnp.float32

time: 574 us -> 517 us (0.901)
  local copies, waits for them, and re-layouts: 108 us -> 53.1 us
  blocking collectives: 86.6 us -> 66.8 us
  waiting for transfers between devices: 274 us -> 291 us
    reshape x1, local copies, waits for them, and re-layouts: 28 us -> 3.66 us  [on_device(): attended = attended.reshape(row_count, frames, col_count, model_width)]
    all_to_all x1 -> x0, local copies, waits for them, and re-layouts: 19.9 us -> none  [on_device(): lax.all_to_all(attended, 'tile', split_axis=3, concat_axis=0, tiled=True)]
    all_to_all x1 -> x0, blocking collectives: 19.8 us -> none  [on_device(): lax.all_to_all(attended, 'tile', split_axis=3, concat_axis=0, tiled=True)]
    unnamed x30 -> x37, local copies, waits for them, and re-layouts: 33.3 us -> 16.9 us
    ppermute x0 -> x3, waiting for transfers between devices: none -> 15.4 us  [on_device(): lax.ppermute(sent, 'tile', [(d, (d + far) % ways) for d in range(ways)])]
  transfers between devices with their start and end apart: 8 -> 11, of which waited for: 6 -> 8; matrix products, arithmetic and copies ran while one was open for 4% -> 5% of each run, Pallas kernels for 0% -> 0%
where the time goes in v1:
time: 517 us; the launch traced here: 516 us
  waiting for transfers between devices  291 us (56%)
  blocking collectives  66.8 us (13%)
  local copies, waits for them, and re-layouts  53.1 us (10%)
  other arithmetic  41.1 us (8%)
  matrix products  39.2 us (8%)
  between operations  15.2 us (3%)
  starting transfers between devices  9.55 us (2%)
    ppermute x1, waiting for transfers between devices, shifted(): return lax.ppermute(x, axis, pairs)  89.7 us
    reduce_scatter x1, waiting for transfers between devices, on_device(): lax.psum_scatter(product.reshape(row_count * lax.axis_size('tile'), frame...  75.3 us
    unnamed x3, blocking collectives  57.1 us
    reduce_scatter x1, waiting for transfers between devices, on_device(): lax.psum_scatter(product.reshape(lax.axis_size('tile') * row_count, frame...  49.1 us
    reduce_scatter x1, waiting for transfers between devices, on_device(): lax.psum_scatter(local_kv, 'tile', scatter_dimension=0, tiled=True)  28.3 us
    all_gather x1, waiting for transfers between devices, on_device(): portion = lax.all_gather(hidden, 'tile', axis=0, tiled=True)  25.9 us
    unnamed x37, local copies, waits for them, and re-layouts  16.9 us
    dot_general x1, matrix products, on_device(): jnp.dot(portion.reshape(-1, model_width), w_flat, preferred_element_type=...  16 us
  transfers between devices with their start and end apart: 11, of which 8 were waited for; matrix products, arithmetic and copies ran while one was open for 5% of the time, Pallas kernels for 0%

profile of v1, /device:TPU:0, one launch (start us, length us, event | category | flops | bytes accessed | tf_op | source)
XLA Modules:
  0.0 516.1 jit_solution(15271110442640914901)
XLA Ops:
  6.5 2.5 broadcast_maximum_fusion
  9.1 4.0 reshape.57
  13.1 4.0 reshape.58
  17.1 3.5 fusion.8
  20.6 28.3 %reduce-scatter.4.cloned.1.call-done = f32[560,112]{1,0:T(8,128)} async-done(((f32[2240,112]{1,0:T(8,128)}), f32[560,112]{1,0:T(8,128)}) %reduce-scatter.4.cloned.1.call-update) | async-done | bytes 250896 | tf_op jit(solution)/shard_map/reduce_scatter | solution.py:77
  48.9 1.5 collective-permute-start
  50.4 7.1 %collective-permute-done = f32[560,112]{1,0:T(8,128)S(1)} collective-permute-done((f32[560,112]{1,0:T(8,128)}, f32[560,112]{1,0:T(8,128)S(1)}, u32[]{:S(2)}, u32[]{:S(2)}) %collective-permute-start) | collective-permute-done | bytes 250912 | tf_op jit(solution)/shard_map/ppermute | solution.py:15
  57.5 1.7 broadcast_multiply_fusion
  59.3 0.6 fusion.17
  60.5 1.5 convert_reduce_fusion
  62.0 10.2 %all-reduce.3 = f32[2240]{0:T(1024)S(1)} all-reduce(f32[2240]{0:T(1024)S(1)} %convert_reduce_fusion), channel_id=5, replica_groups=mesh['blk'=8,'tile'=4] {'tile'}, use_global_device_ids=true, to_apply=%region_2.3.clone | all-reduce | flops 2240 | bytes 17920
  72.2 0.1 dynamic-slice.3
  72.3 1.9 collective-permute-start.1
  74.2 3.0 convert_maximum_fusion
  77.2 0.6 dynamic-slice
  79.0 4.3 reshape.61
  83.3 3.3 copy.27
  86.6 0.2 multiply_dynamic-update-slice_fusion
  86.8 36.8 %all-reduce.1 = f32[4480]{0:T(1024)S(1)} all-reduce(f32[4480]{0:T(1024)S(1)} %multiply_dynamic-update-slice_fusion), channel_id=3, replica_groups=mesh['blk'=8,'tile'=4] {'blk'}, use_global_device_ids=true, to_apply=%add.1 | all-reduce | flops 4480 | bytes 35840
  123.6 0.1 reshape.68
  123.7 8.9 %while.16 = (s32[]{:T(128)}, f32[560,112]{1,0:T(8,128)S(1)}, f32[560]{0:T(1024)S(1)}, s32[]{:T(128)}, f32[8,560,112]{2,1,0:T(8,128)}, /*index=5*/f32[8,560]{1,0:T(8,128)S(1)}, s32[]{:T(128)}, s32[]{:T(128)}) while((s32[]{:T(128)}, f32[560,112]{1,0:T(8,128)S(1)}, f32[560]{0:T(1024)S(1)}, s32[]{:T(128)}, f32[8,560,112]{2,1,0:T(8,128)}, ...), condition=%wide.region_4.5_spmd.clone, body=%wide.region_3.4_spmd.clone.sunk | while | flops 189844 | bytes 763955 | solution.py:30
  123.7 1.1 add_select_fusion.4
  124.9 1.0 add_select_fusion.4
  126.0 1.0 add_select_fusion.4
  127.1 1.0 add_select_fusion.4
  128.2 1.0 add_select_fusion.4
  129.3 1.0 add_select_fusion.4
  130.4 1.0 add_select_fusion.4
  131.5 1.0 add_select_fusion.4
  132.6 0.2 add_dynamic-update-slice_fusion
  132.8 10.1 %all-reduce.2 = f32[2240]{0:T(1024)S(1)} all-reduce(f32[2240]{0:T(1024)S(1)} %add_dynamic-update-slice_fusion), channel_id=1, replica_groups=mesh['blk'=8,'tile'=4] {'tile'}, use_global_device_ids=true, to_apply=%add.2 | all-reduce | flops 2240 | bytes 17920
  142.9 0.1 reshape.84
  143.0 3.0 fusion.18
  146.1 9.7 %all_gather.25 = f32[2240,112]{1,0:T(8,128)S(1)} all-gather(f32[560,112]{1,0:T(8,128)S(1)} %multiply_add_fusion.1), channel_id=1, replica_groups=mesh['blk'=8,'tile'=4] {'tile'}, dimensions={0}, use_global_device_ids=true | all-gather | bytes 1254400 | tf_op jit(solution)/shard_map/all_gather | solution.py:82
  155.9 3.2 fusion.5
  159.0 2.7 copy.28
  161.7 3.7 reshape.63
  165.4 2.6 fusion.12
  168.0 1.0 copy-done.3
  169.0 1.4 fusion.16
  170.4 1.5 collective-permute-start.2
  171.8 0.4 collective-permute-start.3
  172.3 8.0 %collective-permute-done.2 = bf16[8,2,16,560]{3,2,1,0:T(8,128)(2,1)S(1)} collective-permute-done((bf16[8,2,16,560]{3,2,1,0:T(8,128)(2,1)}, bf16[8,2,16,560]{3,2,1,0:T(8,128)(2,1)S(1)}, u32[]{:S(2)}, u32[]{:S(2)}) %collective-permute-start.2) | collective-permute-done | bytes 286752 | tf_op jit(solution)/shard_map/ppermute | solution.py:98
  180.3 7.4 %collective-permute-done.3 = bf16[8,2,16,560]{3,2,1,0:T(8,128)(2,1)S(1)} collective-permute-done((bf16[8,2,16,560]{3,2,1,0:T(8,128)(2,1)}, bf16[8,2,16,560]{3,2,1,0:T(8,128)(2,1)S(1)}, u32[]{:S(2)}, u32[]{:S(2)}) %collective-permute-start.3) | collective-permute-done | bytes 286752 | tf_op jit(solution)/shard_map/ppermute | solution.py:98
  187.8 1.0 constant_dynamic-update-slice_fusion.3
  188.8 1.0 slice_dynamic-update-slice_fusion
  189.9 1.0 constant_dynamic-update-slice_fusion
  190.9 1.0 slice_dynamic-update-slice_fusion.1
  192.0 6.2 %fusion.3 = f32[32,2,16,2240]{3,2,1,0:T(8,128)} fusion(bf16[560,2240]{1,0:T(8,128)(2,1)S(1)} %copy-done, bf16[64,2,16,560]{3,2,1,0:T(8,128)(2,1)S(1)} %slice_dynamic-update-slice_fusion.1, s32[]{:T(128)S(6)} %select_n.71), kind=kOutput, calls=%fused_computation.21 | convolution fusion | flops 2569011200 | bytes 13066244 | tf_op jit(solution)/shard_map/dot_general | solution.py:102
  198.3 75.3 %reduce-scatter.6.cloned.1.call-done = f32[8,2,16,2240]{3,2,1,0:T(8,128)} async-done(((f32[32,2,16,2240]{3,2,1,0:T(8,128)}), f32[8,2,16,2240]{3,2,1,0:T(8,128)}) %reduce-scatter.6.cloned.1.call-update) | async-done | bytes 2293776 | tf_op jit(solution)/shard_map/reduce_scatter | solution.py:105
  273.6 2.9 add_convert_fusion.2
  276.5 0.3 reduce-scatter.8.cloned.1.call-start
  276.8 11.4 %copy.36 = bf16[280,8,2,1024]{3,1,2,0:T(8,128)(2,1)} copy(bf16[280,8,2,1024]{3,2,1,0:T(2,128)(2,1)} %bitcast.81) | data formatting | bytes 18350080
  288.2 25.9 %all-gather.5.cloned.1.call-done = bf16[32,2,16,2240]{3,2,1,0:T(8,128)(2,1)} async-done(((bf16[8,2,16,2240]{3,2,1,0:T(8,128)(2,1)}), bf16[32,2,16,2240]{3,2,1,0:T(8,128)(2,1)}) %all-gather.5.cloned.1.call-update) | async-done | bytes 4587536 | tf_op jit(solution)/shard_map/all_gather | solution.py:114
  314.1 16.0 %multiply_convert_fusion = bf16[1024,2048]{1,0:T(8,128)(2,1)} fusion(bf16[1024,2240]{1,0:T(8,128)(2,1)} %bitcast.86, bf16[2240,2048]{1,0:T(8,128)(2,1)} %bitcast.82), kind=kOutput, calls=%fused_computation.13 | convolution fusion | flops 9405726720 | bytes 17956864 | tf_op jit(solution)/shard_map/dot_general | solution.py:115
  330.1 7.8 %reshape.66 = bf16[32,2,16,2,1024]{4,3,2,1,0:T(2,128)(2,1)} reshape(bf16[1024,2048]{1,0:T(8,128)(2,1)} %multiply_convert_fusion) | data formatting | bytes 8388608 | tf_op jit(solution)/shard_map/reshape | solution.py:117
  337.9 3.5 copy.29
  341.5 11.9 %add_convert_fusion = bf16[32,2,16,2,1024]{4,2,1,0,3:T(8,128)(2,1)S(1)} fusion(bf16[32,2,16,2,1024]{4,2,1,0,3:T(8,128)(2,1)S(1)} %copy.29, f32[2,1024]{1,0:T(2,128)S(1)} %get-tuple-element.160, f32[2,1024]{1,0:T(2,128)S(1)} %get-tuple-element.161, f32[2,1024]{1,0:T(2,128)S(1)} %get-tuple-element.154, f32[2,1024]{1,0:T(2,128)S(1)} %get-tuple-element.155, ...), kind=kLoop, calls=%fused_computation.12 | loop fusion | flops 56623104 | bytes 8462336 | tf_op jit(solution)/shard_map/convert_element_type | solution.py:118
  353.4 3.9 collective-permute-start.5
  357.3 89.7 %collective-permute-done.5 = bf16[32,2,16,2,1024]{4,2,1,0,3:T(8,128)(2,1)S(1)} collective-permute-done((bf16[32,2,16,2,1024]{4,2,1,0,3:T(8,128)(2,1)S(1)}, bf16[32,2,16,2,1024]{4,2,1,0,3:T(8,128)(2,1)S(1)}, u32[]{:S(2)}, u32[]{:S(2)}) %collective-permute-start.5) | collective-permute-done | bytes 4194336 | tf_op jit(solution)/shard_map/ppermute | solution.py:36
  447.0 3.2 multiply_add_fusion
  450.2 7.3 %convolution_convert_fusion = bf16[32,2,16,2240]{3,2,1,0:T(8,128)(2,1)} fusion(bf16[1024,2240]{0,1:T(8,128)(2,1)S(1)} %bitcast.88, f32[32,2,16,2,1024]{4,2,1,0,3:T(8,128)S(1)} %multiply_add_fusion), kind=kOutput, calls=%fused_computation.14 | convolution fusion | flops 4706205696 | bytes 17563648 | tf_op jit(solution)/shard_map/dot_general | solution.py:129
  457.6 49.1 %reduce-scatter.8.cloned.1.call-done = bf16[8,2,16,2240]{3,2,1,0:T(8,128)(2,1)} async-done(((bf16[32,2,16,2240]{3,2,1,0:T(8,128)(2,1)}), bf16[8,2,16,2240]{3,2,1,0:T(8,128)(2,1)}) %reduce-scatter.8.cloned.1.call-update) | async-done | bytes 1146896 | tf_op jit(solution)/shard_map/reduce_scatter | solution.py:130
  506.7 2.9 add_convert_fusion.1
  (65 shorter events, 0.8 us)
Async XLA Ops:
  6.5 185.4 %copy-start = (bf16[560,2240]{1,0:T(8,128)(2,1)S(1)}, bf16[560,2240]{1,0:T(8,128)(2,1)}, u32[]{:S(2)}) copy-start(bf16[560,2240]{1,0:T(8,128)(2,1)} %param.15) | copy-start | bytes 7526404
  6.5 42.4 %reduce-scatter.4.cloned.1.call-start = ((), (), s32[]{:S(2)}) async-start(), calls=%async_computation.3 | async-start | bytes 1433600 | tf_op jit(solution)/shard_map/reduce_scatter | solution.py:77
  17.1 42.2 %copy-start.8 = (u32[32]{0:T(128)S(1)}, u32[32]{0:T(128)}, u32[]{:S(2)}) copy-start(u32[32]{0:T(128)} %constant.122) | copy-start | bytes 388
  20.6 103.1 %all-gather.7.cloned.1.call-start = ((), (), s32[]{:S(2)}) async-start(), calls=%async_computation.7 | async-start | bytes 2580480 | tf_op jit(solution)/shard_map/all_gather | solution.py:20
  48.9 8.6 %collective-permute-start = (f32[560,112]{1,0:T(8,128)}, f32[560,112]{1,0:T(8,128)S(1)}, u32[]{:S(2)}, u32[]{:S(2)}) collective-permute-start(f32[560,112]{1,0:T(8,128)} %reduce-scatter.4.cloned.1.call-done), channel_id=1, source_target_pairs={{0,4},{4,0},{8,12},{12,8},{16,20},{20,16},{24,28},{28,24},{1,5},{5... | collective-permute-start | bytes 752648 | tf_op jit(solution)/shard_map/ppermute | solution.py:15
  59.2 17.9 %copy-start.9 = (u32[32]{0:T(128)S(1)}, u32[32]{0:T(128)}, u32[]{:S(2)}) copy-start(u32[32]{0:T(128)} %constant.117) | copy-start | bytes 388
  59.3 214.3 %reduce-scatter.6.cloned.1.call-start = ((), (), s32[]{:S(2)}) async-start(), calls=%async_computation.4 | async-start | bytes 11796480 | tf_op jit(solution)/shard_map/reduce_scatter | solution.py:105
  72.3 14.3 %collective-permute-start.1 = (f32[560]{0:T(1024)S(1)}, f32[560]{0:T(1024)S(1)}, u32[]{:S(2)}, u32[]{:S(2)}) collective-permute-start(f32[560]{0:T(1024)S(1)} %dynamic-slice.3), channel_id=1, source_target_pairs={{0,4},{4,0},{8,12},{12,8},{16,20},{20,16},{24,28},{28,24},{1,5},{5... | collective-permute-start | bytes 6728 | tf_op jit(solution)/shard_map/ppermute | solution.py:15
  123.7 22.4 %copy-start.5 = (f32[560,112]{1,0:T(8,128)S(1)}, f32[560,112]{1,0:T(8,128)}, u32[]{:S(2)}) copy-start(f32[560,112]{1,0:T(8,128)} %reduce-scatter.4.cloned.1.call-done) | copy-start | bytes 752644
  143.0 12.8 %copy-start.2 = (f32[256,20,112]{0,2,1:T(8,128)S(1)}, f32[256,20,112]{0,2,1:T(8,128)}, u32[]{:S(2)}) copy-start(f32[256,20,112]{0,2,1:T(8,128)} %copy.27) | copy-start | bytes 6881284
  168.0 1.0 copy-start.3
  170.4 9.9 %collective-permute-start.2 = (bf16[8,2,16,560]{3,2,1,0:T(8,128)(2,1)}, bf16[8,2,16,560]{3,2,1,0:T(8,128)(2,1)S(1)}, u32[]{:S(2)}, u32[]{:S(2)}) collective-permute-start(bf16[8,2,16,560]{3,2,1,0:T(8,128)(2,1)} %get-tuple-element.152), channel_id=1, source_target_pairs={{0,3},{1,0},{2,1},{3,2},{4,7},{5,4},{6,5},{7,6},{8,11},{9,8},{10,9... | collective-permute-start | bytes 860168 | tf_op jit(solution)/shard_map/ppermute | solution.py:98
  171.8 15.9 %collective-permute-start.3 = (bf16[8,2,16,560]{3,2,1,0:T(8,128)(2,1)}, bf16[8,2,16,560]{3,2,1,0:T(8,128)(2,1)S(1)}, u32[]{:S(2)}, u32[]{:S(2)}) collective-permute-start(bf16[8,2,16,560]{3,2,1,0:T(8,128)(2,1)} %get-tuple-element.151), channel_id=1, source_target_pairs={{0,2},{1,3},{2,0},{3,1},{4,6},{5,7},{6,4},{7,5},{8,10},{9,11},{10,... | collective-permute-start | bytes 860168 | tf_op jit(solution)/shard_map/ppermute | solution.py:98
  172.3 15.5 %collective-permute-start.4 = (bf16[8,2,16,560]{3,2,1,0:T(8,128)(2,1)}, bf16[8,2,16,560]{3,2,1,0:T(8,128)(2,1)}, u32[]{:S(2)}, u32[]{:S(2)}) collective-permute-start(bf16[8,2,16,560]{3,2,1,0:T(8,128)(2,1)} %get-tuple-element.150), channel_id=1, source_target_pairs={{0,1},{1,2},{2,3},{3,0},{4,5},{5,6},{6,7},{7,4},{8,9},{9,10},{10,1... | collective-permute-start | bytes 860168 | tf_op jit(solution)/shard_map/ppermute | solution.py:98
  198.2 75.4 %copy-start.4 = (bf16[8,2,16,2240]{3,2,1,0:T(8,128)(2,1)S(1)}, bf16[8,2,16,2240]{3,2,1,0:T(8,128)(2,1)}, u32[]{:S(2)}) copy-start(bf16[8,2,16,2240]{3,2,1,0:T(8,128)(2,1)} %param.11) | copy-start | bytes 3440644
  198.2 115.9 %all-gather.5.cloned.1.call-start = ((), (), s32[]{:S(2)}) async-start(), calls=%async_computation.5 | async-start | bytes 5898240 | tf_op jit(solution)/shard_map/all_gather | solution.py:114
  276.5 230.2 %reduce-scatter.8.cloned.1.call-start = ((), (), s32[]{:S(2)}) async-start(), calls=%async_computation.6 | async-start | bytes 5898240 | tf_op jit(solution)/shard_map/reduce_scatter | solution.py:130
  276.8 11.4 %copy-start.6 = (f32[3,3,2,1024]{3,2,1,0:T(2,128)S(1)}, f32[3,3,2,1024]{3,2,1,0:T(2,128)}, u32[]{:S(2)}) copy-start(f32[3,3,2,1024]{3,2,1,0:T(2,128)} %param.18) | copy-start | bytes 221188
  341.5 15.8 %copy-start.7 = (f32[3,2,1024]{2,1,0:T(2,128)S(1)}, f32[3,2,1024]{2,1,0:T(2,128)}, u32[]{:S(2)}) copy-start(f32[3,2,1024]{2,1,0:T(2,128)} %param.19) | copy-start | bytes 73732
  341.5 108.7 %slice-start = ((s8[4587520]{0:T(1024)(128)(4,1)}), s8[4194304]{0:T(1024)(128)(4,1)S(1)}, s32[]{:S(2)}) async-start(s8[4587520]{0:T(1024)(128)(4,1)} %bitcast.87), calls=%async_computation.8 | async-start | bytes 8388608
  353.4 93.6 %collective-permute-start.5 = (bf16[32,2,16,2,1024]{4,2,1,0,3:T(8,128)(2,1)S(1)}, bf16[32,2,16,2,1024]{4,2,1,0,3:T(8,128)(2,1)S(1)}, u32[]{:S(2)}, u32[]{:S(2)}) collective-permute-start(bf16[32,2,16,2,1024]{4,2,1,0,3:T(8,128)(2,1)S(1)} %add_convert_fusion), channel_id=1, source_target_pairs={{0,4},{4,8},{8,12},{12,16},{16,20},{20,24},{24,28},{1,5},{5,9},{9,... | collective-permute-start | bytes 12582920 | tf_op jit(solution)/shard_map/ppermute | solution.py:36
  447.0 3.2 slice-start.1
  457.5 52.0 %copy-start.1 = (bf16[560,2240]{1,0:T(8,128)(2,1)S(1)}, bf16[560,2240]{1,0:T(8,128)(2,1)}, u32[]{:S(2)}) copy-start(bf16[560,2240]{1,0:T(8,128)(2,1)} %param.15) | copy-start | bytes 7526404
Sparse Core Ops, SparseCore 0:
  20.7 28.1 reduce-scatter.3
  59.4 51.6 all-gather.6
  198.3 75.2 reduce-scatter.5
  276.6 37.4 all-gather.4
  457.7 48.9 reduce-scatter.7
